TPU v7x, 32 devices: a whole 2x2x4 slice. The times are simulated.
32 devices in a mesh: ens: 2 (over y), row: 4 (over z), col: 2 (over x), chan: 2 (over core).
Axes of the slice: x: 2, y: 2, z: 4, core: 2. Of those that a mesh axis runs over, the one named last changes fastest.
Arguments:
- latent: float32 [4, 12, 32, 256], P('ens', None, 'row', 'col'), parts along dimension 0, may hold values from -6 to 6
- fresh_noise: float32 [4, 12, 32, 256], P('ens', None, 'row', 'col'), parts along dimension 0, may hold values from -6 to 6
- step_index: int32 [4], P('ens'), parts along dimension 0, may hold values from 0 to 11
- coarse: float32 [24, 4, 32], P('ens', None, 'col'), parts along dimension 0, may hold values from -6 to 6
- weight_in: bfloat16 [9, 256, 24], replicated, may hold values from -0.4375 to 0.4375
- bias_in: float32 [256], replicated, may hold values from -4 to 4
- weight_noise: float32 [256], replicated, may hold values from -4 to 4
- weight_mid: bfloat16 [9, 256, 256], P(None, 'chan'), may hold values from -0.125 to 0.125
- bias_mid: float32 [256], P('chan'), may hold values from -4 to 4
- weight_out: bfloat16 [12, 256], P(None, 'chan'), may hold values from -0.375 to 0.375
Outputs:
- fine_field: float32 [4, 12, 32, 256], P('ens', None, 'row', 'col'), parts along dimension 0
- next_latent: float32 [4, 12, 32, 256], P('ens', None, 'row', 'col'), parts along dimension 0
There are 2 independent parts, one for each index of `ens`. A program takes and returns all parts, laid end to end along the dimension named above; an argument that names none is the same for every part. Nothing has to cross between parts.
Inputs may be any that keep to these rules, and one draw needn't show every extreme that they name: `step_index`: each sample's position in the noise plan of 18 steps.
All inputs are finite; a program needn't handle non-finite values.
Results may differ from a plain program's by a relative error of at most 0.0024.
Values may be sent and summed in bfloat16 or wider, within the bound.
No kernel may reach another device: no remote copies, remote signals or barrier semaphores. Data moves between devices by JAX's collectives and lax.ppermute only.
A program may use at most 64 MiB of HBM per device.

v0:
```python
import jax
import jax.numpy as jnp
from jax import lax
from jax.sharding import PartitionSpec as P

STEPS = 18
FACTOR = 8
sigma_data = 0.5
sigma_high = 80.0
sigma_low = 0.002
rho_power = 7.0


def extended_2(value, sides, width):
    for axis, dim in sides:
        count, length = (lax.axis_size(axis), value.shape[dim])
        up = [(i, (i + 1) % count) for i in range(count - 1)]
        down = [(j, i) for i, j in up]
        last = lax.slice_in_dim(value, length - width, length, axis=dim)
        initial = lax.slice_in_dim(value, 0, width, axis=dim)
        before = lax.ppermute(last, axis, up)
        after = lax.ppermute(initial, axis, down)
        value = jnp.concatenate([before, value, after], axis=dim)
    return value


def blend_matrix(fine_index, coarse_index, coarse_count, factor):
    twice_pos = 2 * fine_index + 1 - factor
    lower_cell = twice_pos // (2 * factor)
    fraction = (twice_pos - lower_cell * 2 * factor).astype(jnp.float32) / (2.0 * factor)
    before = lower_cell < 0
    fraction = jnp.where(before, 0.0, fraction)
    lower_clip = jnp.clip(lower_cell, 0, coarse_count - 1)
    upper_clip = jnp.clip(lower_cell + 1, 0, coarse_count - 1)
    lower_hit = (lower_clip[:, None] == coarse_index[None, :]).astype(jnp.float32)
    upper_hit = (upper_clip[:, None] == coarse_index[None, :]).astype(jnp.float32)
    return (1.0 - fraction)[:, None] * lower_hit + fraction[:, None] * upper_hit


def noise_level(position):
    top_root = sigma_high ** (1.0 / rho_power)
    bottom_root = sigma_low ** (1.0 / rho_power)
    along = position.astype(jnp.float32) / (STEPS - 1)
    return (top_root + along * (bottom_root - top_root)) ** rho_power


def conv_valid(source, weight, out_rows, out_cols):
    total = None
    for offset_row in range(3):
        for offset_col in range(3):
            window = source[
                :, :, offset_row : offset_row + out_rows, offset_col : offset_col + out_cols
            ]
            term = jnp.einsum(
                "oi,siyx->soyx",
                weight[3 * offset_row + offset_col],
                window,
                preferred_element_type=jnp.float32,
            )
            total = term if total is None else total + term
    return total


def on_device(
    latent,
    fresh_noise,
    step_index,
    coarse,
    weight_in,
    bias_in,
    weight_noise,
    weight_mid,
    bias_mid,
    weight_out,
):
    samples, channels, rows_here, cols_here = latent.shape
    row_place = lax.axis_index("row")
    col_place = lax.axis_index("col")
    height = lax.axis_size("row") * rows_here
    width = lax.axis_size("col") * cols_here
    coarse_rows = coarse.shape[1]
    local_cols = coarse.shape[2]
    coarse_cols = lax.axis_size("col") * local_cols
    widened = extended_2(coarse, (("col", 2),), 1)
    rows_matrix = blend_matrix(
        row_place * rows_here + jnp.arange(rows_here, dtype=jnp.int32),
        jnp.arange(coarse_rows, dtype=jnp.int32),
        coarse_rows,
        FACTOR,
    )
    cols_matrix = blend_matrix(
        col_place * cols_here + jnp.arange(cols_here, dtype=jnp.int32),
        col_place * local_cols - 1 + jnp.arange(local_cols + 2, dtype=jnp.int32),
        coarse_cols,
        FACTOR,
    )
    mean_up = jnp.einsum(
        "yh,khw,xw->kyx", rows_matrix, widened, cols_matrix, precision=lax.Precision.HIGHEST
    )
    noise_now = noise_level(step_index)
    noise_next = noise_level(step_index + 1)
    inputs = jnp.concatenate(
        [latent, jnp.broadcast_to(mean_up[None], (samples,) + mean_up.shape)], axis=1
    ).astype(jnp.bfloat16)
    conditioning = (
        bias_in[None, :, None, None]
        + (jnp.log(noise_now) / 4.0)[:, None, None, None] * weight_noise[None, :, None, None]
    )
    mid_full, out_full = (
        lax.all_gather(weight_mid, "chan", axis=1, tiled=True),
        lax.all_gather(weight_out, "chan", axis=1, tiled=True),
    )
    bias_full = lax.all_gather(bias_mid, "chan", axis=0, tiled=True)
    half_cols = cols_here // lax.axis_size("chan")
    chan_place = lax.axis_index("chan")
    extended = extended_2(inputs, (("row", 2), ("col", 3)), 2)
    source = lax.dynamic_slice_in_dim(extended, chan_place * half_cols, half_cols + 4, 3)
    hidden = jax.nn.silu(conv_valid(source, weight_in, rows_here + 2, half_cols + 2) + conditioning)
    global_rows = row_place * rows_here - 1 + jnp.arange(rows_here + 2, dtype=jnp.int32)
    global_cols = (
        col_place * cols_here
        + chan_place * half_cols
        - 1
        + jnp.arange(half_cols + 2, dtype=jnp.int32)
    )
    inside = ((global_rows >= 0) & (global_rows < height))[:, None] & (
        (global_cols >= 0) & (global_cols < width)
    )[None, :]
    hidden_wide = jnp.where(inside, hidden, 0.0).astype(jnp.bfloat16)
    middle = jax.nn.silu(
        conv_valid(hidden_wide, mid_full, rows_here, half_cols) + bias_full[None, :, None, None]
    ).astype(jnp.bfloat16)
    half_network = jnp.einsum("ko,soyx->skyx", out_full, middle, preferred_element_type=jnp.float32)
    network = lax.all_gather(half_network, "chan", axis=3, tiled=True)
    scale_now = jnp.sqrt(noise_now * noise_now + sigma_data * sigma_data)
    skip_coef = sigma_data * sigma_data / (noise_now * noise_now + sigma_data * sigma_data)
    out_coef = sigma_data * noise_now / scale_now
    denoised = (skip_coef * scale_now)[:, None, None, None] * latent + out_coef[
        :, None, None, None
    ] * network
    fine_field = mean_up[None] + denoised
    scale_next = jnp.sqrt(noise_next * noise_next + sigma_data * sigma_data)
    next_latent = (denoised + noise_next[:, None, None, None] * fresh_noise) / scale_next[
        :, None, None, None
    ]
    return (fine_field, next_latent)


def solution(mesh):
    in_specs = (
        P("ens", None, "row", "col"),
        P("ens", None, "row", "col"),
        P("ens"),
        P("ens", None, "col"),
        P(),
        P(),
        P(),
        P(None, "chan", None),
        P("chan"),
        P(None, "chan"),
    )
    out_specs = (P("ens", None, "row", "col"), P("ens", None, "row", "col"))
    return jax.shard_map(
        on_device, mesh=mesh, in_specs=in_specs, out_specs=out_specs, check_vma=False
    )
```

profile of v0, /device:TPU:0, one launch (start us, length us, event | category | flops | bytes accessed | tf_op | source)
XLA Modules:
  0.0 60.4 jit_solution(1089614030091482770)
XLA Ops:
  7.2 0.7 %copy.29 = f32[12,4,16]{2,0,1:T(8,128)S(1)} copy(f32[12,4,16]{2,1,0:T(4,128)} %param.13) | data formatting | bytes 6144 | tf_op args[3]
  8.0 4.9 %collective-permute-start = (f32[12,4,1]{2,0,1:T(8,128)S(1)}, f32[12,4,1]{2,0,1:T(8,128)S(1)}, u32[]{:S(2)}, u32[]{:S(2)}) collective-permute-start(f32[12,4,1]{2,0,1:T(8,128)S(1)} %get-tuple-element.23), channel_id=1, source_target_pairs={{0,2},{1,3},{4,6},{5,7},{8,10},{9,11},{12,14},{13,15},{16,18},{17,... | collective-permute-start | bytes 584 | tf_op jit(solution)/shard_map/ppermute | solution.py:21
  12.9 1.3 %collective-permute-start.1 = (f32[12,4,1]{2,0,1:T(8,128)S(1)}, f32[12,4,1]{2,0,1:T(8,128)S(1)}, u32[]{:S(2)}, u32[]{:S(2)}) collective-permute-start(f32[12,4,1]{2,0,1:T(8,128)S(1)} %get-tuple-element.24), channel_id=1, source_target_pairs={{2,0},{3,1},{6,4},{7,5},{10,8},{11,9},{14,12},{15,13},{18,16},{19,... | collective-permute-start | bytes 584 | tf_op jit(solution)/shard_map/ppermute | solution.py:22
  14.4 0.8 %add_sqrt_fusion = (f32[2]{0:T(128)S(1)}, f32[2]{0:T(128)S(1)}, f32[2]{0:T(128)S(1)}, f32[2]{0:T(128)S(1)}, f32[2]{0:T(128)S(1)}) fusion(s32[2]{0:T(128)} %param.12), kind=kLoop, calls=%fused_computation.139 | loop fusion | flops 34 | bytes 48 | tf_op jit(solution)/shard_map/sqrt | solution.py:142
  15.1 0.8 %multiply_add_fusion.1 = f32[2,256]{1,0:T(2,128)S(1)} fusion(f32[256]{0:T(256)} %param.16, f32[256]{0:T(256)} %param.15, f32[2]{0:T(128)S(1)} %get-tuple-element.25), kind=kLoop, calls=%fused_computation.115 | loop fusion | flops 1024 | bytes 4104 | tf_op jit(solution)/shard_map/add | solution.py:106
  15.9 0.9 %convert.7 = bf16[2,12,8,128]{3,2,1,0:T(8,128)(2,1)S(1)} convert(f32[2,12,8,128]{3,2,1,0:T(8,128)} %param.10) | non-fusion elementwise | flops 24576 | bytes 147456 | tf_op jit(solution)/shard_map/convert
  16.8 1.9 %collective-permute-done.1 = f32[12,4,1]{2,0,1:T(8,128)S(1)} collective-permute-done((f32[12,4,1]{2,0,1:T(8,128)S(1)}, f32[12,4,1]{2,0,1:T(8,128)S(1)}, u32[]{:S(2)}, u32[]{:S(2)}) %collective-permute-start.1) | collective-permute-done | bytes 224 | tf_op jit(solution)/shard_map/ppermute | solution.py:22
  19.3 3.5 %collective-permute-start.2 = (bf16[2,24,2,128]{3,2,1,0:T(2,128)(2,1)S(1)}, bf16[2,24,2,128]{3,2,1,0:T(2,128)(2,1)S(1)}, u32[]{:S(2)}, u32[]{:S(2)}) collective-permute-start(bf16[2,24,2,128]{3,2,1,0:T(2,128)(2,1)S(1)} %get-tuple-element.21), channel_id=1, source_target_pairs={{0,4},{4,8},{8,12},{1,5},{5,9},{9,13},{2,6},{6,10},{10,14},{3,7},{... | collective-permute-start | bytes 73736 | tf_op jit(solution)/shard_map/ppermute | solution.py:21
  22.8 1.3 %collective-permute-start.3 = (bf16[2,24,2,128]{3,2,1,0:T(2,128)(2,1)S(1)}, bf16[2,24,2,128]{3,2,1,0:T(2,128)(2,1)S(1)}, u32[]{:S(2)}, u32[]{:S(2)}) collective-permute-start(bf16[2,24,2,128]{3,2,1,0:T(2,128)(2,1)S(1)} %get-tuple-element.22), channel_id=1, source_target_pairs={{4,0},{8,4},{12,8},{5,1},{9,5},{13,9},{6,2},{10,6},{14,10},{7,3},{... | collective-permute-start | bytes 73736 | tf_op jit(solution)/shard_map/ppermute | solution.py:22
  24.3 4.2 %collective-permute-done.3 = bf16[2,24,2,128]{3,2,1,0:T(2,128)(2,1)S(1)} collective-permute-done((bf16[2,24,2,128]{3,2,1,0:T(2,128)(2,1)S(1)}, bf16[2,24,2,128]{3,2,1,0:T(2,128)(2,1)S(1)}, u32[]{:S(2)}, u32[]{:S(2)}) %collective-permute-start.3) | collective-permute-done | bytes 24608 | tf_op jit(solution)/shard_map/ppermute | solution.py:22
  28.7 2.6 %collective-permute-start.4 = (bf16[2,24,12,2]{3,2,1,0:T(8,128)(2,1)S(1)}, bf16[2,24,12,2]{3,2,1,0:T(8,128)(2,1)S(1)}, u32[]{:S(2)}, u32[]{:S(2)}) collective-permute-start(bf16[2,24,12,2]{3,2,1,0:T(8,128)(2,1)S(1)} %get-tuple-element.20), channel_id=1, source_target_pairs={{0,2},{1,3},{4,6},{5,7},{8,10},{9,11},{12,14},{13,15},{16,18},{17,... | collective-permute-start | bytes 6920 | tf_op jit(solution)/shard_map/ppermute | solution.py:21
  31.4 1.3 %collective-permute-start.5 = (bf16[2,24,12,2]{3,2,1,0:T(8,128)(2,1)S(1)}, bf16[2,24,12,2]{3,2,1,0:T(8,128)(2,1)S(1)}, u32[]{:S(2)}, u32[]{:S(2)}) collective-permute-start(bf16[2,24,12,2]{3,2,1,0:T(8,128)(2,1)S(1)} %get-tuple-element.19), channel_id=1, source_target_pairs={{2,0},{3,1},{6,4},{7,5},{10,8},{11,9},{14,12},{15,13},{18,16},{19,... | collective-permute-start | bytes 6920 | tf_op jit(solution)/shard_map/ppermute | solution.py:22
  32.8 1.8 %all-gather = f32[2,1,128]{2,1,0:T(1,128)S(1)} all-gather(f32[1,1,128]{2,1,0:T(1,128)S(1)} %bitcast.167), channel_id=1, replica_groups=mesh['ens'=2,'row'=4,'col'=2,'chan'=2] {'chan'}, dimensions={0}, use_global_device_ids=true | all-gather | bytes 1536 | tf_op jit(solution)/shard_map/all_gather | solution.py:113
  34.6 1.8 %all_gather.14 = bf16[12,256]{1,0:T(8,128)(2,1)S(1)} all-gather(bf16[12,128]{1,0:T(8,128)(2,1)S(1)} %copy-done.4), channel_id=1, replica_groups=mesh['ens'=2,'row'=4,'col'=2,'chan'=2] {'chan'}, dimensions={1}, use_global_device_ids=true | all-gather | bytes 9216 | tf_op jit(solution)/shard_map/all_gather | solution.py:111
  36.4 2.6 %collective-permute-done.5 = bf16[2,24,12,2]{3,2,1,0:T(8,128)(2,1)S(1)} collective-permute-done((bf16[2,24,12,2]{3,2,1,0:T(8,128)(2,1)S(1)}, bf16[2,24,12,2]{3,2,1,0:T(8,128)(2,1)S(1)}, u32[]{:S(2)}, u32[]{:S(2)}) %collective-permute-start.5) | collective-permute-done | bytes 2336 | tf_op jit(solution)/shard_map/ppermute | solution.py:22
  39.0 0.6 %fusion.21 = bf16[2,24,12,68]{3,2,1,0:T(8,128)(2,1)S(1)} fusion(s32[]{:T(128)S(6)} %select_n.69, bf16[2,24,12,2]{3,2,1,0:T(8,128)(2,1)S(1)} %collective-permute-done.4, bf16[2,24,2,128]{3,2,1,0:T(2,128)(2,1)S(1)} %collective-permute-done.2, bf16[2,12,8,128]{3,2,1,0:T(8,128)(2,1)S(1)} %convert.7, bf16[2,12,8,128]{3,2,1,0:T(8,128)(2,1)S(1)} %add.314, ...), kind=kLoop, calls=%fused_computation.39 | loop fusion | flops 470016 | bytes 230404 | tf_op jit(solution)/shard_map/concatenate | solution.py:23
  39.6 0.5 fusion.93
  40.1 0.4 copy-done.2
  40.5 0.4 fusion.26
  40.9 0.4 fusion.28
  41.3 0.4 fusion.30
  41.7 0.4 fusion.32
  42.1 0.4 fusion.34
  42.5 0.4 fusion.36
  42.9 0.4 fusion.38
  43.3 0.4 fusion.40
  43.7 1.0 %fusion.4 = bf16[2,256,10,66]{1,3,2,0:T(8,128)(2,1)S(1)} fusion(f32[2,10,66,256]{3,2,1,0:T(8,128)S(1)} %fusion.26, f32[2,10,66,256]{3,2,1,0:T(8,128)S(1)} %fusion.28, f32[2,10,66,256]{3,2,1,0:T(8,128)S(1)} %fusion.30, f32[2,10,66,256]{3,2,1,0:T(8,128)S(1)} %fusion.32, f32[2,10,66,256]{3,2,1,0:T(8,128)S(1)} %fusion.34, f32[2,10,66,256]{3,2,1,0:T(8,128)S(1)} %fusion.36, ...), kind=kOutput, calls=%fused_computation.6 | convolution fusion | flops 21288960 | bytes 12685312 | tf_op jit(solution)/shard_map/oi,siyx->soyx/dot_general | solution.py:54
  44.8 1.3 %fusion.16 = f32[2,8,64,256]{3,2,1,0:T(8,128)S(1)} fusion(bf16[2,256,10,66]{1,3,2,0:T(8,128)(2,1)S(1)} %fusion.4, bf16[9,256,256]{2,1,0:T(8,128)(2,1)} %all-gather.3.cloned.1.call-done), kind=kOutput, calls=%fused_computation.28 | convolution fusion | flops 134217728 | bytes 1703936 | tf_op jit(solution)/shard_map/oi,siyx->soyx/dot_general | solution.py:54
  48.6 0.7 %convolution_bitcast_fusion = f32[2,12,8,64]{3,1,2,0:T(8,128)S(1)} fusion(f32[2,8,64,256]{3,2,1,0:T(8,128)S(1)} %convolution_add_fusion.1, bf16[2,256,10,66]{1,3,2,0:T(8,128)(2,1)S(1)} %fusion.4, f32[256]{0:T(256)S(1)} %bitcast.168, bf16[9,256,256]{2,1,0:T(8,128)(2,1)S(1)} %copy-done, bf16[12,256]{1,0:T(8,128)(2,1)S(1)} %all_gather.14), kind=kOutput, calls=%fused_computation.17 | convolution fusion | flops 142344192 | bytes 1762304 | tf_op jit(solution)/shard_map/ko,soyx->skyx/dot_general | solution.py:133
  49.7 2.7 %all_gather.15 = f32[2,12,8,128]{1,2,0,3:T(8,128)S(1)} all-gather(f32[2,12,8,64]{1,2,0,3:T(8,128)S(1)} %copy.42), channel_id=1, replica_groups=mesh['ens'=2,'row'=4,'col'=2,'chan'=2] {'chan'}, dimensions={3}, use_global_device_ids=true | all-gather | bytes 147456 | tf_op jit(solution)/shard_map/all_gather | solution.py:134
  52.4 0.4 copy.43
  52.8 0.8 %add_divide_fusion = (f32[2,12,8,128]{3,2,1,0:T(8,128)}, f32[2,12,8,128]{3,2,1,0:T(8,128)}) fusion(f32[2,12,8,128]{3,2,1,0:T(8,128)S(1)} %copy-done.3, f32[2]{0:T(128)S(1)} %get-tuple-element.6, f32[2]{0:T(128)S(1)} %get-tuple-element.7, f32[2,12,8,128]{3,2,1,0:T(8,128)S(1)} %copy.43, f32[2]{0:T(128)S(1)} %get-tuple-element.26, ...), kind=kLoop, calls=%fused_computation.70 | loop fusion | flops 172032 | bytes 540704 | tf_op jit(solution)/shard_map/div | solution.py:143
  (40 shorter events, 4.0 us)
Async XLA Ops:
  7.2 25.6 %copy-start.5 = (f32[128]{0:T(128)S(1)}, f32[128]{0:T(128)}, u32[]{:S(2)}) copy-start(f32[128]{0:T(128)} %param.18) | copy-start | bytes 1540
  7.2 27.4 %copy-start.4 = (bf16[12,128]{1,0:T(8,128)(2,1)S(1)}, bf16[12,128]{1,0:T(8,128)(2,1)}, u32[]{:S(2)}) copy-start(bf16[12,128]{1,0:T(8,128)(2,1)} %param.19) | copy-start | bytes 9220
  7.2 37.6 %all-gather.3.cloned.1.call-start = ((), (), s32[]{:S(2)}) async-start(), calls=%async_computation | async-start | bytes 1769472 | tf_op jit(solution)/shard_map/all_gather | solution.py:110
  8.0 8.8 %collective-permute-start = (f32[12,4,1]{2,0,1:T(8,128)S(1)}, f32[12,4,1]{2,0,1:T(8,128)S(1)}, u32[]{:S(2)}, u32[]{:S(2)}) collective-permute-start(f32[12,4,1]{2,0,1:T(8,128)S(1)} %get-tuple-element.23), channel_id=1, source_target_pairs={{0,2},{1,3},{4,6},{5,7},{8,10},{9,11},{12,14},{13,15},{16,18},{17,... | collective-permute-start | bytes 584 | tf_op jit(solution)/shard_map/ppermute | solution.py:21
  12.9 5.8 %collective-permute-start.1 = (f32[12,4,1]{2,0,1:T(8,128)S(1)}, f32[12,4,1]{2,0,1:T(8,128)S(1)}, u32[]{:S(2)}, u32[]{:S(2)}) collective-permute-start(f32[12,4,1]{2,0,1:T(8,128)S(1)} %get-tuple-element.24), channel_id=1, source_target_pairs={{2,0},{3,1},{6,4},{7,5},{10,8},{11,9},{14,12},{15,13},{18,16},{19,... | collective-permute-start | bytes 584 | tf_op jit(solution)/shard_map/ppermute | solution.py:22
  19.3 5.0 %collective-permute-start.2 = (bf16[2,24,2,128]{3,2,1,0:T(2,128)(2,1)S(1)}, bf16[2,24,2,128]{3,2,1,0:T(2,128)(2,1)S(1)}, u32[]{:S(2)}, u32[]{:S(2)}) collective-permute-start(bf16[2,24,2,128]{3,2,1,0:T(2,128)(2,1)S(1)} %get-tuple-element.21), channel_id=1, source_target_pairs={{0,4},{4,8},{8,12},{1,5},{5,9},{9,13},{2,6},{6,10},{10,14},{3,7},{... | collective-permute-start | bytes 73736 | tf_op jit(solution)/shard_map/ppermute | solution.py:21
  22.8 5.7 %collective-permute-start.3 = (bf16[2,24,2,128]{3,2,1,0:T(2,128)(2,1)S(1)}, bf16[2,24,2,128]{3,2,1,0:T(2,128)(2,1)S(1)}, u32[]{:S(2)}, u32[]{:S(2)}) collective-permute-start(bf16[2,24,2,128]{3,2,1,0:T(2,128)(2,1)S(1)} %get-tuple-element.22), channel_id=1, source_target_pairs={{4,0},{8,4},{12,8},{5,1},{9,5},{13,9},{6,2},{10,6},{14,10},{7,3},{... | collective-permute-start | bytes 73736 | tf_op jit(solution)/shard_map/ppermute | solution.py:22
  28.7 7.7 %collective-permute-start.4 = (bf16[2,24,12,2]{3,2,1,0:T(8,128)(2,1)S(1)}, bf16[2,24,12,2]{3,2,1,0:T(8,128)(2,1)S(1)}, u32[]{:S(2)}, u32[]{:S(2)}) collective-permute-start(bf16[2,24,12,2]{3,2,1,0:T(8,128)(2,1)S(1)} %get-tuple-element.20), channel_id=1, source_target_pairs={{0,2},{1,3},{4,6},{5,7},{8,10},{9,11},{12,14},{13,15},{16,18},{17,... | collective-permute-start | bytes 6920 | tf_op jit(solution)/shard_map/ppermute | solution.py:21
  31.4 7.6 %collective-permute-start.5 = (bf16[2,24,12,2]{3,2,1,0:T(8,128)(2,1)S(1)}, bf16[2,24,12,2]{3,2,1,0:T(8,128)(2,1)S(1)}, u32[]{:S(2)}, u32[]{:S(2)}) collective-permute-start(bf16[2,24,12,2]{3,2,1,0:T(8,128)(2,1)S(1)} %get-tuple-element.19), channel_id=1, source_target_pairs={{2,0},{3,1},{6,4},{7,5},{10,8},{11,9},{14,12},{15,13},{18,16},{19,... | collective-permute-start | bytes 6920 | tf_op jit(solution)/shard_map/ppermute | solution.py:22
  39.6 0.9 %copy-start.2 = (bf16[9,256,24]{1,2,0:T(8,128)(2,1)S(1)}, bf16[9,256,24]{1,2,0:T(8,128)(2,1)}, u32[]{:S(2)}) copy-start(bf16[9,256,24]{1,2,0:T(8,128)(2,1)} %param.14) | copy-start | bytes 331780
  44.8 1.3 %copy-start = (bf16[9,256,256]{2,1,0:T(8,128)(2,1)S(1)}, bf16[9,256,256]{2,1,0:T(8,128)(2,1)}, u32[]{:S(2)}) copy-start(bf16[9,256,256]{2,1,0:T(8,128)(2,1)} %all-gather.3.cloned.1.call-done) | copy-start | bytes 3538948
  49.7 3.2 %copy-start.1 = (f32[2,12,8,128]{3,2,1,0:T(8,128)S(1)}, f32[2,12,8,128]{3,2,1,0:T(8,128)}, u32[]{:S(2)}) copy-start(f32[2,12,8,128]{3,2,1,0:T(8,128)} %param.10) | copy-start | bytes 294916
  49.7 3.1 %copy-start.3 = (f32[2,12,8,128]{3,2,1,0:T(8,128)S(1)}, f32[2,12,8,128]{3,2,1,0:T(8,128)}, u32[]{:S(2)}) copy-start(f32[2,12,8,128]{3,2,1,0:T(8,128)} %param.11) | copy-start | bytes 294916
Sparse Core Ops, SparseCore 0:
  14.4 11.6 all-gather.2
where the time goes:
time: 60.9 us; the launch traced here: 60.4 us
  starting transfers between devices  14.9 us (24%)
  between operations  14.4 us (24%)
  matrix products  9.14 us (15%)
  waiting for transfers between devices  8.92 us (15%)
  blocking collectives  6.31 us (10%)
  other arithmetic  4.14 us (7%)
  local copies, waits for them, and re-layouts  2.63 us (4%)
    ppermute x3, starting transfers between devices, extended_2(): before = lax.ppermute(last, axis, up)  11 us
    ppermute x3, waiting for transfers between devices, extended_2(): after = lax.ppermute(initial, axis, down)  8.69 us
    dot_general x17, matrix products, conv_valid(): jnp.einsum('oi,siyx->soyx', weight[3 * offset_row + offset_col], window,...  7.96 us
    ppermute x3, starting transfers between devices, extended_2(): after = lax.ppermute(initial, axis, down)  3.88 us
    all_gather x1, blocking collectives, on_device(): network = lax.all_gather(half_network, 'chan', axis=3, tiled=True)  2.69 us
    all_gather x1, blocking collectives, on_device(): lax.all_gather(weight_out, 'chan', axis=1, tiled=True)  1.83 us
    all_gather x1, blocking collectives, on_device(): bias_full = lax.all_gather(bias_mid, 'chan', axis=0, tiled=True)  1.8 us
  transfers between devices with their start and end apart: 7, of which 4 were waited for; matrix products, arithmetic and copies ran while one was open for 14% of the time, Pallas kernels for 0%

commit v1 on v0

--- a/solution.py
+++ b/solution.py
@@ -131,7 +131,15 @@
         conv_valid(hidden_wide, mid_full, rows_here, half_cols) + bias_full[None, :, None, None]
     ).astype(jnp.bfloat16)
     half_network = jnp.einsum("ko,soyx->skyx", out_full, middle, preferred_element_type=jnp.float32)
-    network = lax.all_gather(half_network, "chan", axis=3, tiled=True)
+    network = jnp.concatenate(
+        lax.all_to_all(
+            jnp.stack(lax.axis_size("chan") * [half_network]),
+            axis_name="chan",
+            split_axis=0,
+            concat_axis=0,
+        ),
+        3,
+    )
     scale_now = jnp.sqrt(noise_now * noise_now + sigma_data * sigma_data)
     skip_coef = sigma_data * sigma_data / (noise_now * noise_now + sigma_data * sigma_data)
     out_coef = sigma_data * noise_now / scale_now

time: 60.9 us -> 63.4 us (1.041)
  blocking collectives: 6.31 us -> 7.42 us
  other arithmetic: 4.14 us -> 5.12 us
    all_to_all x0 -> x1, blocking collectives: none -> 3.79 us  [on_device(): lax.all_to_all(jnp.stack(lax.axis_size('chan') * [half_network]), axis_na...]
    all_gather x1 -> x0, blocking collectives: 2.69 us -> none  [on_device(): network = lax.all_gather(half_network, 'chan', axis=3, tiled=True)]
    all_to_all x0 -> x1, other arithmetic: none -> 0.94 us  [on_device(): lax.all_to_all(jnp.stack(lax.axis_size('chan') * [half_network]), axis_na...]
    unnamed x13 -> x15, local copies, waits for them, and re-layouts: 1.2 us -> 1.52 us
where the time goes in v1:
time: 63.4 us; the launch traced here: 63 us
  starting transfers between devices  14.9 us (24%)
  between operations  14.4 us (23%)
  matrix products  9.14 us (14%)
  waiting for transfers between devices  8.92 us (14%)
  blocking collectives  7.42 us (12%)
  other arithmetic  5.12 us (8%)
  local copies, waits for them, and re-layouts  3.06 us (5%)
    ppermute x3, starting transfers between devices, extended_2(): before = lax.ppermute(last, axis, up)  11 us
    ppermute x3, waiting for transfers between devices, extended_2(): after = lax.ppermute(initial, axis, down)  8.69 us
    dot_general x17, matrix products, conv_valid(): jnp.einsum('oi,siyx->soyx', weight[3 * offset_row + offset_col], window,...  7.96 us
    ppermute x3, starting transfers between devices, extended_2(): after = lax.ppermute(initial, axis, down)  3.88 us
    all_to_all x1, blocking collectives, on_device(): lax.all_to_all(jnp.stack(lax.axis_size('chan') * [half_network]), axis_na...  3.79 us
    all_gather x1, blocking collectives, on_device(): lax.all_gather(weight_out, 'chan', axis=1, tiled=True)  1.83 us
    all_gather x1, blocking collectives, on_device(): bias_full = lax.all_gather(bias_mid, 'chan', axis=0, tiled=True)  1.8 us
    unnamed x15, local copies, waits for them, and re-layouts  1.52 us
  transfers between devices with their start and end apart: 7, of which 4 were waited for; matrix products, arithmetic and copies ran while one was open for 14% of the time, Pallas kernels for 0%

profile of v1, /device:TPU:0, one launch (start us, length us, event | category | flops | bytes accessed | tf_op | source)
XLA Modules:
  0.0 63.0 jit_solution(5564194359743422021)
XLA Ops:
  7.2 0.7 %copy.25 = f32[12,4,16]{2,0,1:T(8,128)S(1)} copy(f32[12,4,16]{2,1,0:T(4,128)} %param.13) | data formatting | bytes 6144 | tf_op args[3]
  8.0 4.9 %collective-permute-start = (f32[12,4,1]{2,0,1:T(8,128)S(1)}, f32[12,4,1]{2,0,1:T(8,128)S(1)}, u32[]{:S(2)}, u32[]{:S(2)}) collective-permute-start(f32[12,4,1]{2,0,1:T(8,128)S(1)} %get-tuple-element.19), channel_id=1, source_target_pairs={{0,2},{1,3},{4,6},{5,7},{8,10},{9,11},{12,14},{13,15},{16,18},{17,... | collective-permute-start | bytes 584 | tf_op jit(solution)/shard_map/ppermute | solution.py:21
  12.9 1.3 %collective-permute-start.1 = (f32[12,4,1]{2,0,1:T(8,128)S(1)}, f32[12,4,1]{2,0,1:T(8,128)S(1)}, u32[]{:S(2)}, u32[]{:S(2)}) collective-permute-start(f32[12,4,1]{2,0,1:T(8,128)S(1)} %get-tuple-element.20), channel_id=1, source_target_pairs={{2,0},{3,1},{6,4},{7,5},{10,8},{11,9},{14,12},{15,13},{18,16},{19,... | collective-permute-start | bytes 584 | tf_op jit(solution)/shard_map/ppermute | solution.py:22
  14.4 0.8 %add_sqrt_fusion = (f32[2]{0:T(128)S(1)}, f32[2]{0:T(128)S(1)}, f32[2]{0:T(128)S(1)}, f32[2]{0:T(128)S(1)}, f32[2]{0:T(128)S(1)}) fusion(s32[2]{0:T(128)} %param.12), kind=kLoop, calls=%fused_computation.140 | loop fusion | flops 34 | bytes 48 | tf_op jit(solution)/shard_map/sqrt | solution.py:150
  15.1 0.8 %multiply_add_fusion.1 = f32[2,256]{1,0:T(2,128)S(1)} fusion(f32[256]{0:T(256)} %param.16, f32[256]{0:T(256)} %param.15, f32[2]{0:T(128)S(1)} %get-tuple-element.21), kind=kLoop, calls=%fused_computation.116 | loop fusion | flops 1024 | bytes 4104 | tf_op jit(solution)/shard_map/add | solution.py:106
  15.9 0.9 %convert.7 = bf16[2,12,8,128]{3,2,1,0:T(8,128)(2,1)S(1)} convert(f32[2,12,8,128]{3,2,1,0:T(8,128)} %param.10) | non-fusion elementwise | flops 24576 | bytes 147456 | tf_op jit(solution)/shard_map/convert
  16.8 1.9 %collective-permute-done.1 = f32[12,4,1]{2,0,1:T(8,128)S(1)} collective-permute-done((f32[12,4,1]{2,0,1:T(8,128)S(1)}, f32[12,4,1]{2,0,1:T(8,128)S(1)}, u32[]{:S(2)}, u32[]{:S(2)}) %collective-permute-start.1) | collective-permute-done | bytes 224 | tf_op jit(solution)/shard_map/ppermute | solution.py:22
  19.3 3.5 %collective-permute-start.2 = (bf16[2,24,2,128]{3,2,1,0:T(2,128)(2,1)S(1)}, bf16[2,24,2,128]{3,2,1,0:T(2,128)(2,1)S(1)}, u32[]{:S(2)}, u32[]{:S(2)}) collective-permute-start(bf16[2,24,2,128]{3,2,1,0:T(2,128)(2,1)S(1)} %get-tuple-element.17), channel_id=1, source_target_pairs={{0,4},{4,8},{8,12},{1,5},{5,9},{9,13},{2,6},{6,10},{10,14},{3,7},{... | collective-permute-start | bytes 73736 | tf_op jit(solution)/shard_map/ppermute | solution.py:21
  22.8 1.3 %collective-permute-start.3 = (bf16[2,24,2,128]{3,2,1,0:T(2,128)(2,1)S(1)}, bf16[2,24,2,128]{3,2,1,0:T(2,128)(2,1)S(1)}, u32[]{:S(2)}, u32[]{:S(2)}) collective-permute-start(bf16[2,24,2,128]{3,2,1,0:T(2,128)(2,1)S(1)} %get-tuple-element.18), channel_id=1, source_target_pairs={{4,0},{8,4},{12,8},{5,1},{9,5},{13,9},{6,2},{10,6},{14,10},{7,3},{... | collective-permute-start | bytes 73736 | tf_op jit(solution)/shard_map/ppermute | solution.py:22
  24.3 4.2 %collective-permute-done.3 = bf16[2,24,2,128]{3,2,1,0:T(2,128)(2,1)S(1)} collective-permute-done((bf16[2,24,2,128]{3,2,1,0:T(2,128)(2,1)S(1)}, bf16[2,24,2,128]{3,2,1,0:T(2,128)(2,1)S(1)}, u32[]{:S(2)}, u32[]{:S(2)}) %collective-permute-start.3) | collective-permute-done | bytes 24608 | tf_op jit(solution)/shard_map/ppermute | solution.py:22
  28.7 2.6 %collective-permute-start.4 = (bf16[2,24,12,2]{3,2,1,0:T(8,128)(2,1)S(1)}, bf16[2,24,12,2]{3,2,1,0:T(8,128)(2,1)S(1)}, u32[]{:S(2)}, u32[]{:S(2)}) collective-permute-start(bf16[2,24,12,2]{3,2,1,0:T(8,128)(2,1)S(1)} %get-tuple-element.16), channel_id=1, source_target_pairs={{0,2},{1,3},{4,6},{5,7},{8,10},{9,11},{12,14},{13,15},{16,18},{17,... | collective-permute-start | bytes 6920 | tf_op jit(solution)/shard_map/ppermute | solution.py:21
  31.4 1.3 %collective-permute-start.5 = (bf16[2,24,12,2]{3,2,1,0:T(8,128)(2,1)S(1)}, bf16[2,24,12,2]{3,2,1,0:T(8,128)(2,1)S(1)}, u32[]{:S(2)}, u32[]{:S(2)}) collective-permute-start(bf16[2,24,12,2]{3,2,1,0:T(8,128)(2,1)S(1)} %get-tuple-element.15), channel_id=1, source_target_pairs={{2,0},{3,1},{6,4},{7,5},{10,8},{11,9},{14,12},{15,13},{18,16},{19,... | collective-permute-start | bytes 6920 | tf_op jit(solution)/shard_map/ppermute | solution.py:22
  32.8 1.8 %all-gather = f32[2,1,128]{2,1,0:T(1,128)S(1)} all-gather(f32[1,1,128]{2,1,0:T(1,128)S(1)} %bitcast.171), channel_id=1, replica_groups=mesh['ens'=2,'row'=4,'col'=2,'chan'=2] {'chan'}, dimensions={0}, use_global_device_ids=true | all-gather | bytes 1536 | tf_op jit(solution)/shard_map/all_gather | solution.py:113
  34.6 1.8 %all_gather.11 = bf16[12,256]{1,0:T(8,128)(2,1)S(1)} all-gather(bf16[12,128]{1,0:T(8,128)(2,1)S(1)} %copy-done.4), channel_id=1, replica_groups=mesh['ens'=2,'row'=4,'col'=2,'chan'=2] {'chan'}, dimensions={1}, use_global_device_ids=true | all-gather | bytes 9216 | tf_op jit(solution)/shard_map/all_gather | solution.py:111
  36.4 2.6 %collective-permute-done.5 = bf16[2,24,12,2]{3,2,1,0:T(8,128)(2,1)S(1)} collective-permute-done((bf16[2,24,12,2]{3,2,1,0:T(8,128)(2,1)S(1)}, bf16[2,24,12,2]{3,2,1,0:T(8,128)(2,1)S(1)}, u32[]{:S(2)}, u32[]{:S(2)}) %collective-permute-start.5) | collective-permute-done | bytes 2336 | tf_op jit(solution)/shard_map/ppermute | solution.py:22
  39.0 0.6 %fusion.21 = bf16[2,24,12,68]{3,2,1,0:T(8,128)(2,1)S(1)} fusion(s32[]{:T(128)S(6)} %select_n.69, bf16[2,24,12,2]{3,2,1,0:T(8,128)(2,1)S(1)} %collective-permute-done.4, bf16[2,24,2,128]{3,2,1,0:T(2,128)(2,1)S(1)} %collective-permute-done.2, bf16[2,12,8,128]{3,2,1,0:T(8,128)(2,1)S(1)} %convert.7, bf16[2,12,8,128]{3,2,1,0:T(8,128)(2,1)S(1)} %add.314, ...), kind=kLoop, calls=%fused_computation.40 | loop fusion | flops 470016 | bytes 230404 | tf_op jit(solution)/shard_map/concatenate | solution.py:23
  39.6 0.5 fusion.93
  40.1 0.4 copy-done.2
  40.5 0.4 fusion.26
  40.9 0.4 fusion.28
  41.3 0.4 fusion.30
  41.7 0.4 fusion.32
  42.1 0.4 fusion.34
  42.5 0.4 fusion.36
  42.9 0.4 fusion.38
  43.7 1.0 %fusion.4 = bf16[2,256,10,66]{1,3,2,0:T(8,128)(2,1)S(1)} fusion(f32[2,10,66,256]{3,2,1,0:T(8,128)S(1)} %fusion.26, f32[2,10,66,256]{3,2,1,0:T(8,128)S(1)} %fusion.28, f32[2,10,66,256]{3,2,1,0:T(8,128)S(1)} %fusion.30, f32[2,10,66,256]{3,2,1,0:T(8,128)S(1)} %fusion.32, f32[2,10,66,256]{3,2,1,0:T(8,128)S(1)} %fusion.34, f32[2,10,66,256]{3,2,1,0:T(8,128)S(1)} %fusion.36, ...), kind=kOutput, calls=%fused_computation.6 | convolution fusion | flops 21288960 | bytes 12685312 | tf_op jit(solution)/shard_map/oi,siyx->soyx/dot_general | solution.py:54
  44.8 1.3 %fusion.16 = f32[2,8,64,256]{3,2,1,0:T(8,128)S(1)} fusion(bf16[2,256,10,66]{1,3,2,0:T(8,128)(2,1)S(1)} %fusion.4, bf16[9,256,256]{2,1,0:T(8,128)(2,1)} %all-gather.3.cloned.1.call-done), kind=kOutput, calls=%fused_computation.28 | convolution fusion | flops 134217728 | bytes 1703936 | tf_op jit(solution)/shard_map/oi,siyx->soyx/dot_general | solution.py:54
  48.6 0.7 %convolution_bitcast_fusion = f32[1,2,12,8,64]{4,2,3,1,0:T(8,128)S(1)} fusion(f32[2,8,64,256]{3,2,1,0:T(8,128)S(1)} %convolution_add_fusion.1, bf16[2,256,10,66]{1,3,2,0:T(8,128)(2,1)S(1)} %fusion.4, f32[256]{0:T(256)S(1)} %bitcast.172, bf16[9,256,256]{2,1,0:T(8,128)(2,1)S(1)} %copy-done, bf16[12,256]{1,0:T(8,128)(2,1)S(1)} %all_gather.11), kind=kOutput, calls=%fused_computation.17 | convolution fusion | flops 142344192 | bytes 1762304 | tf_op jit(solution)/shard_map/ko,soyx->skyx/dot_general | solution.py:133
  49.6 3.8 %all_to_all.5 = f32[2,1,12288]{2,1,0:T(1,128)S(1)} all-to-all(f32[2,1,12288]{2,1,0:T(1,128)S(1)} %reshape.180), channel_id=1, replica_groups=mesh['ens'=2,'row'=4,'col'=2,'chan'=2] {'chan'}, dimensions={0} | all-to-all | bytes 196608 | tf_op jit(solution)/shard_map/all_to_all | solution.py:135
  53.4 0.5 broadcast.638
  53.9 0.9 %reduce = f32[2,12288]{1,0:T(2,128)S(1)} reduce(f32[2,1,12288]{2,1,0:T(1,128)S(1)} %all_to_all.5, f32[]{:T(128)} %broadcast.638), dimensions={1}, to_apply=%all_to_all.3.reduce_sub_computation | reduce | bytes 196612 | tf_op jit(solution)/shard_map/all_to_all | solution.py:135
  55.3 0.8 %add_divide_fusion = (f32[2,12,8,128]{3,2,1,0:T(8,128)}, f32[2,12,8,128]{3,2,1,0:T(8,128)}) fusion(f32[2,12,8,128]{3,2,1,0:T(8,128)S(1)} %copy-done.3, f32[2]{0:T(128)S(1)} %get-tuple-element.2, f32[2]{0:T(128)S(1)} %get-tuple-element.3, f32[2,12,8,128]{3,2,1,0:T(8,128)S(1)} %reshape.156, f32[2]{0:T(128)S(1)} %get-tuple-element.22, ...), kind=kLoop, calls=%fused_computation.71 | loop fusion | flops 172032 | bytes 540704 | tf_op jit(solution)/shard_map/div | solution.py:151
  (46 shorter events, 4.8 us)
Async XLA Ops:
  7.2 25.6 %copy-start.5 = (f32[128]{0:T(128)S(1)}, f32[128]{0:T(128)}, u32[]{:S(2)}) copy-start(f32[128]{0:T(128)} %param.18) | copy-start | bytes 1540
  7.2 27.4 %copy-start.4 = (bf16[12,128]{1,0:T(8,128)(2,1)S(1)}, bf16[12,128]{1,0:T(8,128)(2,1)}, u32[]{:S(2)}) copy-start(bf16[12,128]{1,0:T(8,128)(2,1)} %param.19) | copy-start | bytes 9220
  7.2 37.6 %all-gather.3.cloned.1.call-start = ((), (), s32[]{:S(2)}) async-start(), calls=%async_computation.1 | async-start | bytes 1769472 | tf_op jit(solution)/shard_map/all_gather | solution.py:110
  8.0 8.8 %collective-permute-start = (f32[12,4,1]{2,0,1:T(8,128)S(1)}, f32[12,4,1]{2,0,1:T(8,128)S(1)}, u32[]{:S(2)}, u32[]{:S(2)}) collective-permute-start(f32[12,4,1]{2,0,1:T(8,128)S(1)} %get-tuple-element.19), channel_id=1, source_target_pairs={{0,2},{1,3},{4,6},{5,7},{8,10},{9,11},{12,14},{13,15},{16,18},{17,... | collective-permute-start | bytes 584 | tf_op jit(solution)/shard_map/ppermute | solution.py:21
  12.9 5.8 %collective-permute-start.1 = (f32[12,4,1]{2,0,1:T(8,128)S(1)}, f32[12,4,1]{2,0,1:T(8,128)S(1)}, u32[]{:S(2)}, u32[]{:S(2)}) collective-permute-start(f32[12,4,1]{2,0,1:T(8,128)S(1)} %get-tuple-element.20), channel_id=1, source_target_pairs={{2,0},{3,1},{6,4},{7,5},{10,8},{11,9},{14,12},{15,13},{18,16},{19,... | collective-permute-start | bytes 584 | tf_op jit(solution)/shard_map/ppermute | solution.py:22
  19.3 5.0 %collective-permute-start.2 = (bf16[2,24,2,128]{3,2,1,0:T(2,128)(2,1)S(1)}, bf16[2,24,2,128]{3,2,1,0:T(2,128)(2,1)S(1)}, u32[]{:S(2)}, u32[]{:S(2)}) collective-permute-start(bf16[2,24,2,128]{3,2,1,0:T(2,128)(2,1)S(1)} %get-tuple-element.17), channel_id=1, source_target_pairs={{0,4},{4,8},{8,12},{1,5},{5,9},{9,13},{2,6},{6,10},{10,14},{3,7},{... | collective-permute-start | bytes 73736 | tf_op jit(solution)/shard_map/ppermute | solution.py:21
  22.8 5.7 %collective-permute-start.3 = (bf16[2,24,2,128]{3,2,1,0:T(2,128)(2,1)S(1)}, bf16[2,24,2,128]{3,2,1,0:T(2,128)(2,1)S(1)}, u32[]{:S(2)}, u32[]{:S(2)}) collective-permute-start(bf16[2,24,2,128]{3,2,1,0:T(2,128)(2,1)S(1)} %get-tuple-element.18), channel_id=1, source_target_pairs={{4,0},{8,4},{12,8},{5,1},{9,5},{13,9},{6,2},{10,6},{14,10},{7,3},{... | collective-permute-start | bytes 73736 | tf_op jit(solution)/shard_map/ppermute | solution.py:22
  28.7 7.7 %collective-permute-start.4 = (bf16[2,24,12,2]{3,2,1,0:T(8,128)(2,1)S(1)}, bf16[2,24,12,2]{3,2,1,0:T(8,128)(2,1)S(1)}, u32[]{:S(2)}, u32[]{:S(2)}) collective-permute-start(bf16[2,24,12,2]{3,2,1,0:T(8,128)(2,1)S(1)} %get-tuple-element.16), channel_id=1, source_target_pairs={{0,2},{1,3},{4,6},{5,7},{8,10},{9,11},{12,14},{13,15},{16,18},{17,... | collective-permute-start | bytes 6920 | tf_op jit(solution)/shard_map/ppermute | solution.py:21
  31.4 7.6 %collective-permute-start.5 = (bf16[2,24,12,2]{3,2,1,0:T(8,128)(2,1)S(1)}, bf16[2,24,12,2]{3,2,1,0:T(8,128)(2,1)S(1)}, u32[]{:S(2)}, u32[]{:S(2)}) collective-permute-start(bf16[2,24,12,2]{3,2,1,0:T(8,128)(2,1)S(1)} %get-tuple-element.15), channel_id=1, source_target_pairs={{2,0},{3,1},{6,4},{7,5},{10,8},{11,9},{14,12},{15,13},{18,16},{19,... | collective-permute-start | bytes 6920 | tf_op jit(solution)/shard_map/ppermute | solution.py:22
  39.6 0.9 %copy-start.2 = (bf16[9,256,24]{1,2,0:T(8,128)(2,1)S(1)}, bf16[9,256,24]{1,2,0:T(8,128)(2,1)}, u32[]{:S(2)}) copy-start(bf16[9,256,24]{1,2,0:T(8,128)(2,1)} %param.14) | copy-start | bytes 331780
  44.8 1.3 %copy-start = (bf16[9,256,256]{2,1,0:T(8,128)(2,1)S(1)}, bf16[9,256,256]{2,1,0:T(8,128)(2,1)}, u32[]{:S(2)}) copy-start(bf16[9,256,256]{2,1,0:T(8,128)(2,1)} %all-gather.3.cloned.1.call-done) | copy-start | bytes 3538948
  49.3 6.0 %copy-start.1 = (f32[2,12,8,128]{3,2,1,0:T(8,128)S(1)}, f32[2,12,8,128]{3,2,1,0:T(8,128)}, u32[]{:S(2)}) copy-start(f32[2,12,8,128]{3,2,1,0:T(8,128)} %param.10) | copy-start | bytes 294916
  49.3 6.0 %copy-start.3 = (f32[2,12,8,128]{3,2,1,0:T(8,128)S(1)}, f32[2,12,8,128]{3,2,1,0:T(8,128)}, u32[]{:S(2)}) copy-start(f32[2,12,8,128]{3,2,1,0:T(8,128)} %param.11) | copy-start | bytes 294916
Sparse Core Ops, SparseCore 0:
  14.4 11.6 all-gather.2
